TPU v7x, 32 devices: a whole 2x2x4 slice. The times are simulated.
32 devices in a mesh: ckpt: 4 (over z), shard: 8 (over y, x, core).
Axes of the slice: x: 2, y: 2, z: 4, core: 2. Of those that a mesh axis runs over, the one named last changes fastest.
Arguments:
- task_vectors: bfloat16 [4, 4096, 16384], P('ckpt', 'shard'), may hold values from -0.125 to 0.125, as said below
- thresholds: float32 [4], replicated, may hold values from 0.009 to 0.062, as said below
- base_weight: float32 [4096, 16384], P('ckpt', 'shard'), may hold values from -0.3 to 0.3
Outputs:
- merged: float32 [4096, 16384], P('ckpt', 'shard')
Inputs may be any that keep to these rules, and one draw needn't show every extreme that they name: `task_vectors`: every entry is a whole multiple of 2^-14. `thresholds`: every threshold is an odd multiple of 2^-15.
All inputs are finite; a program needn't handle non-finite values.
Results may differ from a plain program's by a relative error of at most 0.0003.
Values may be sent and summed in bfloat16 or wider, within the bound.
A program may use at most 128 MiB of HBM per device.

v0:
```python
import jax
import jax.numpy as jnp
from jax import lax
from jax.sharding import PartitionSpec as P


def local_mean(all_tasks, limits):
    values = all_tasks.astype(jnp.float32)
    trimmed = jnp.where(jnp.abs(values) > limits[:, None, None], values, jnp.float32(0.0))
    signed_total = jnp.sum(trimmed, axis=0)
    agreeing = jnp.logical_or(
        jnp.logical_and(signed_total[None] > 0, trimmed > 0),
        jnp.logical_and(signed_total[None] < 0, trimmed < 0),
    )
    kept_sum = jnp.sum(jnp.where(agreeing, trimmed, jnp.float32(0.0)), axis=0)
    agree_count = jnp.sum(agreeing.astype(jnp.float32), axis=0)
    return jnp.where(agree_count > 0, kept_sum / jnp.maximum(agree_count, 1.0), jnp.float32(0.0))


def local(task_vectors, thresholds, base_weight):
    ckpt_count = lax.axis_size("ckpt")
    shard_count = lax.axis_size("shard")
    all_tasks = lax.all_to_all(task_vectors, "ckpt", split_axis=1, concat_axis=0, tiled=True)
    mean_part = local_mean(all_tasks, thresholds)
    block_rows = mean_part.shape[0]
    by_columns = lax.all_to_all(mean_part, "shard", split_axis=1, concat_axis=0, tiled=True)
    col_width = by_columns.shape[1]
    by_rows = lax.all_to_all(by_columns, "ckpt", split_axis=0, concat_axis=0, tiled=True)
    group_size = shard_count // ckpt_count
    disjoint = by_rows.reshape(ckpt_count, group_size, block_rows, col_width)
    disjoint = disjoint.transpose(1, 0, 2, 3).reshape(
        group_size * ckpt_count * block_rows, col_width
    )
    return base_weight + disjoint


def solution(mesh):
    placed = (P("ckpt", "shard", None), P(), P("ckpt", "shard"))
    return jax.shard_map(
        local, mesh=mesh, in_specs=placed, out_specs=P("ckpt", "shard"), check_vma=False
    )
```

profile of v0, /device:TPU:0, one launch (start us, length us, event | category | flops | bytes accessed | tf_op | source)
XLA Modules:
  0.0 955.8 jit_solution(856141177414765462)
XLA Ops:
  0.0 29.1 %copy.18 = bf16[1,512,16384]{2,0,1:T(2,128)(2,1)} copy(bf16[1,512,16384]{2,1,0:T(8,128)(2,1)} %param.3) | data formatting | bytes 33554432 | tf_op args[0]
  29.1 0.5 broadcast.94
  29.6 99.6 %reduce = bf16[512,16384]{1,0:T(8,128)(2,1)} reduce(bf16[512,1,16384]{2,1,0:T(2,128)(2,1)} %bitcast.16, bf16[]{:T(256)} %broadcast.94), dimensions={1}, to_apply=%bitcast.13.reduce_sub_computation | reduce | bytes 33554432
  129.3 17.4 %reshape.60 = bf16[4,2,1048576]{2,1,0:T(2,128)(2,1)} reshape(bf16[512,16384]{1,0:T(8,128)(2,1)} %reduce) | data formatting | bytes 33554432
  146.6 375.8 %all_to_all.31 = bf16[4,2,1048576]{2,1,0:T(2,128)(2,1)} all-to-all(bf16[4,2,1048576]{2,1,0:T(2,128)(2,1)} %reshape.60), channel_id=1, replica_groups=mesh['ckpt'=4,'shard'=8] {'ckpt'}, dimensions={0} | all-to-all | bytes 33554432 | tf_op jit(solution)/shard_map/all_to_all | solution.py:23
  522.4 35.6 %reshape.61 = bf16[512,1,16384]{2,1,0:T(2,128)(2,1)} reshape(bf16[4,2,1048576]{2,1,0:T(2,128)(2,1)} %all_to_all.31) | data formatting | bytes 33554432
  558.0 0.0 copy-start
  558.1 28.2 %copy.13 = bf16[1,512,16384]{2,1,0:T(8,128)(2,1)S(1)} copy(bf16[1,512,16384]{2,0,1:T(2,128)(2,1)} %bitcast.17) | data formatting | bytes 33554432 | tf_op jit(solution)/shard_map/all_to_all | solution.py:23
  586.3 0.0 copy-done
  586.3 13.3 %fusion.3 = f32[128,16384]{1,0:T(8,128)S(1)} fusion(bf16[4,128,16384]{2,1,0:T(8,128)(2,1)S(1)} %bitcast.14, f32[4]{0:T(128)S(1)} %copy-done), kind=kLoop, calls=%fused_computation.5 | loop fusion | flops 39845888 | bytes 25165840 | tf_op jit(solution)/shard_map/reduce_sum | solution.py:10
  599.6 3.8 broadcast_compare_fusion.1
  603.4 25.8 %convert_reduce_fusion = (f32[128,16384]{1,0:T(8,128)S(1)}, f32[128,16384]{1,0:T(8,128)}) fusion(f32[4]{0:T(128)S(1)} %copy-done, bf16[4,128,16384]{2,1,0:T(8,128)(2,1)S(1)} %bitcast.15, pred[128,16384]{1,0:T(8,128)(4,1)} %get-tuple-element.8, pred[128,16384]{1,0:T(8,128)(4,1)} %get-tuple-element.7), kind=kLoop, calls=%fused_computation.8 | loop fusion | flops 104857600 | bytes 37748752 | tf_op jit(solution)/shard_map/reduce_sum | solution.py:16
  629.1 6.3 divide_select_fusion
  635.4 9.0 copy.14
  644.4 99.7 %all_to_all.32 = f32[128,8,2048]{0,2,1:T(8,128)} all-to-all(f32[128,8,2048]{0,2,1:T(8,128)} %bitcast.18), channel_id=1, replica_groups=mesh['ckpt'=4,'shard'=8] {'shard'}, dimensions={1} | all-to-all | bytes 16777216 | tf_op jit(solution)/shard_map/all_to_all | solution.py:26
  744.1 9.1 copy.15
  753.3 186.9 %all_to_all.33 = f32[4,256,2048]{2,1,0:T(8,128)S(1)} all-to-all(f32[4,256,2048]{2,1,0:T(8,128)} %bitcast.20), channel_id=1, replica_groups=mesh['ckpt'=4,'shard'=8] {'ckpt'}, dimensions={0} | all-to-all | bytes 16777216 | tf_op jit(solution)/shard_map/all_to_all | solution.py:28
  940.1 3.8 copy.16
  943.9 11.9 %bitcast_add_fusion = f32[1024,2048]{1,0:T(8,128)} fusion(f32[1024,2048]{1,0:T(8,128)} %param.5, f32[2,4,128,2048]{3,2,1,0:T(8,128)} %copy.16), kind=kLoop, calls=%fused_computation.12 | loop fusion | flops 2097152 | bytes 25165824 | tf_op jit(solution)/shard_map/add | solution.py:34
Async XLA Ops:
  558.0 28.3 %copy-start = (f32[4]{0:T(128)S(1)}, f32[4]{0:T(128)}, u32[]{:S(2)}) copy-start(f32[4]{0:T(128)} %param.4) | copy-start | bytes 52
where the time goes:
time: 957 us; the launch traced here: 956 us
  blocking collectives  662 us (69%)
  other arithmetic  161 us (17%)
  local copies, waits for them, and re-layouts  133 us (14%)
    all_to_all x1, blocking collectives, local(): lax.all_to_all(task_vectors, 'ckpt', split_axis=1, concat_axis=0, tiled=T...  376 us
    all_to_all x1, blocking collectives, local(): lax.all_to_all(by_columns, 'ckpt', split_axis=0, concat_axis=0, tiled=True)  187 us
    all_to_all x1, blocking collectives, local(): lax.all_to_all(mean_part, 'shard', split_axis=1, concat_axis=0, tiled=True)  99.7 us
    unnamed x1, other arithmetic  99.6 us
    unnamed x6, local copies, waits for them, and re-layouts  82.6 us
    all_to_all x1, local copies, waits for them, and re-layouts, local(): lax.all_to_all(task_vectors, 'ckpt', split_axis=1, concat_axis=0, tiled=T...  28.2 us
    reduce_sum x1, other arithmetic, local_mean(): agree_count = jnp.sum(agreeing.astype(jnp.float32), axis=0)  25.8 us

commit v1 on v0

--- a/solution.py
+++ b/solution.py
@@ -23,7 +23,12 @@
     all_tasks = lax.all_to_all(task_vectors, "ckpt", split_axis=1, concat_axis=0, tiled=True)
     mean_part = local_mean(all_tasks, thresholds)
     block_rows = mean_part.shape[0]
-    by_columns = lax.all_to_all(mean_part, "shard", split_axis=1, concat_axis=0, tiled=True)
+    by_columns = jnp.concatenate(
+        lax.all_to_all(
+            jnp.stack(jnp.split(mean_part, lax.axis_size("shard"), axis=1)), "shard", 0, 0
+        ),
+        axis=0,
+    )
     col_width = by_columns.shape[1]
     by_rows = lax.all_to_all(by_columns, "ckpt", split_axis=0, concat_axis=0, tiled=True)
     group_size = shard_count // ckpt_count

time: 957 us -> 933 us (0.975)
  local copies, waits for them, and re-layouts: 133 us -> 115 us
    unnamed x6 -> x13, local copies, waits for them, and re-layouts: 82.6 us -> 83.2 us
where the time goes in v1:
time: 933 us
  blocking collectives  659 us (71%)
  other arithmetic  158 us (17%)
  local copies, waits for them, and re-layouts  115 us (12%)
    all_to_all x1, blocking collectives, local(): lax.all_to_all(task_vectors, 'ckpt', split_axis=1, concat_axis=0, tiled=T...  376 us
    all_to_all x1, blocking collectives, local(): lax.all_to_all(by_columns, 'ckpt', split_axis=0, concat_axis=0, tiled=True)  185 us
    unnamed x1, other arithmetic  99.6 us
    all_to_all x1, blocking collectives, local(): lax.all_to_all(jnp.stack(jnp.split(mean_part, lax.axis_size('shard'), axi...  97.5 us
    unnamed x13, local copies, waits for them, and re-layouts  83.2 us
    all_to_all x1, local copies, waits for them, and re-layouts, local(): lax.all_to_all(task_vectors, 'ckpt', split_axis=1, concat_axis=0, tiled=T...  28.2 us
    reduce_sum x1, other arithmetic, local_mean(): agree_count = jnp.sum(agreeing.astype(jnp.float32), axis=0)  25.8 us

profile of v1, /device:TPU:0, one launch (start us, length us, event | category | flops | bytes accessed | tf_op | source)
XLA Modules:
  0.0 932.6 jit_solution(4184166912658508664)
XLA Ops:
  0.0 29.1 %copy.11 = bf16[1,512,16384]{2,0,1:T(2,128)(2,1)} copy(bf16[1,512,16384]{2,1,0:T(8,128)(2,1)} %param.3) | data formatting | bytes 33554432 | tf_op args[0]
  29.1 0.5 broadcast.85
  29.6 99.6 %reduce = bf16[512,16384]{1,0:T(8,128)(2,1)} reduce(bf16[512,1,16384]{2,1,0:T(2,128)(2,1)} %bitcast.46, bf16[]{:T(256)} %broadcast.85), dimensions={1}, to_apply=%bitcast.43.reduce_sub_computation | reduce | bytes 33554432
  129.3 17.4 %reshape.49 = bf16[4,2,1048576]{2,1,0:T(2,128)(2,1)} reshape(bf16[512,16384]{1,0:T(8,128)(2,1)} %reduce) | data formatting | bytes 33554432
  146.6 375.8 %all_to_all.23 = bf16[4,2,1048576]{2,1,0:T(2,128)(2,1)} all-to-all(bf16[4,2,1048576]{2,1,0:T(2,128)(2,1)} %reshape.49), channel_id=1, replica_groups=mesh['ckpt'=4,'shard'=8] {'ckpt'}, dimensions={0} | all-to-all | bytes 33554432 | tf_op jit(solution)/shard_map/all_to_all | solution.py:23
  522.4 35.6 %reshape.50 = bf16[512,1,16384]{2,1,0:T(2,128)(2,1)} reshape(bf16[4,2,1048576]{2,1,0:T(2,128)(2,1)} %all_to_all.23) | data formatting | bytes 33554432
  558.1 28.2 %copy.8 = bf16[1,512,16384]{2,1,0:T(8,128)(2,1)S(1)} copy(bf16[1,512,16384]{2,0,1:T(2,128)(2,1)} %bitcast.47) | data formatting | bytes 33554432 | tf_op jit(solution)/shard_map/all_to_all | solution.py:23
  586.3 0.0 copy-done
  586.3 13.3 %fusion.3 = f32[128,16384]{1,0:T(8,128)S(1)} fusion(bf16[4,128,16384]{2,1,0:T(8,128)(2,1)S(1)} %bitcast.44, f32[4]{0:T(128)S(1)} %copy-done), kind=kLoop, calls=%fused_computation.5 | loop fusion | flops 39845888 | bytes 25165840 | tf_op jit(solution)/shard_map/reduce_sum | solution.py:10
  599.6 3.8 broadcast_compare_fusion.1
  603.4 25.8 %convert_reduce_fusion = (f32[128,16384]{1,0:T(8,128)S(1)}, f32[128,16384]{1,0:T(8,128)}) fusion(f32[4]{0:T(128)S(1)} %copy-done, bf16[4,128,16384]{2,1,0:T(8,128)(2,1)S(1)} %bitcast.45, pred[128,16384]{1,0:T(8,128)(4,1)} %get-tuple-element.8, pred[128,16384]{1,0:T(8,128)(4,1)} %get-tuple-element.7), kind=kLoop, calls=%fused_computation.8 | loop fusion | flops 104857600 | bytes 37748752 | tf_op jit(solution)/shard_map/reduce_sum | solution.py:16
  629.1 4.2 divide_select_fusion
  633.3 0.1 fusion.16
  633.4 0.1 fusion.15
  633.5 0.1 fusion.14
  633.6 0.1 fusion.13
  633.6 0.1 fusion.12
  633.7 0.1 fusion.11
  633.8 0.1 fusion.10
  633.9 0.1 fusion.9
  634.0 97.5 %all_to_all.24 = f32[8,128,2048]{2,1,0:T(8,128)S(1)} all-to-all(f32[8,128,2048]{2,1,0:T(8,128)S(1)} %fusion.9), channel_id=1, replica_groups=mesh['ckpt'=4,'shard'=8] {'shard'}, dimensions={0} | all-to-all | bytes 16777216 | tf_op jit(solution)/shard_map/all_to_all | solution.py:27
  731.5 185.5 %all_to_all.25 = f32[4,256,2048]{2,1,0:T(8,128)S(1)} all-to-all(f32[4,256,2048]{2,1,0:T(8,128)S(1)} %bitcast.48), channel_id=1, replica_groups=mesh['ckpt'=4,'shard'=8] {'ckpt'}, dimensions={0} | all-to-all | bytes 16777216 | tf_op jit(solution)/shard_map/all_to_all | solution.py:33
  917.0 3.8 copy.9
  920.8 11.9 %bitcast_add_fusion = f32[1024,2048]{1,0:T(8,128)} fusion(f32[1024,2048]{1,0:T(8,128)} %param.5, f32[2,4,128,2048]{3,2,1,0:T(8,128)} %copy.9), kind=kLoop, calls=%fused_computation.12 | loop fusion | flops 2097152 | bytes 25165824 | tf_op jit(solution)/shard_map/add | solution.py:39
  (1 shorter events, 0.0 us)
Async XLA Ops:
  558.0 28.3 %copy-start = (f32[4]{0:T(128)S(1)}, f32[4]{0:T(128)}, u32[]{:S(2)}) copy-start(f32[4]{0:T(128)} %param.4) | copy-start | bytes 52
